TPU v7x, 256 devices: a whole 4x4x8 slice. The times are simulated.
256 devices in a mesh: row: 16 (over z, core), col: 4 (over x), inner: 4 (over y).
Axes of the slice: x: 4, y: 4, z: 8, core: 2. Of those that a mesh axis runs over, the one named last changes fastest.
Arguments:
- density: bfloat16 [64, 16, 256, 256], P('row', ('col', 'inner')), may hold values from -1.5 to 1.5, as said below
- block_cols: int32 [64, 16], replicated, may hold values from 0 to 63, as said below
- mixing: float32 [3], replicated, may hold values from 0.02 to 1.5, as said below
Outputs:
- purified: bfloat16 [64, 16, 256, 256], P('row', ('col', 'inner'))
Inputs may be any that keep to these rules, and one draw needn't show every extreme that they name: Slot g of block row i names a block row of group g (rows g * 4 to g * 4 + 3); within one group of block rows, slot g names each row of group g once. Slot i // 4 of row i names i itself. The pattern is symmetric: row block_cols[i, g] names i in slot i // 4. It is consistent: block_cols[block_cols[i, t], g] == block_cols[i, g] for all i, t, g. `density`: block (i, g) is the transpose of block (block_cols[i, g], i // 4). `mixing`: element 0 lies in 0.5 to 1.5, elements 1 and 2 in 0.02 to 0.05.
All inputs are finite; a program needn't handle non-finite values.
Results may differ from a plain program's by a relative error of at most 0.007.
Values may be sent and summed in bfloat16 or wider, within the bound.
No kernel may reach another device: no remote copies, remote signals or barrier semaphores. Data moves between devices by JAX's collectives and lax.ppermute only.
A program may use at most 128 MiB of HBM per device.

v0:
```python
import jax
import jax.numpy as jnp
from jax import lax
from jax.sharding import PartitionSpec as P

GS = 4


def laid_out(tiles, dim):
    tiles = jnp.moveaxis(tiles, 0, dim)
    shape = tiles.shape
    return tiles.reshape(*shape[:dim], shape[dim] * shape[dim + 1], *shape[dim + 2 :])


def from_everyone(shard, axis):
    size = lax.axis_size(axis)
    return lax.all_to_all(
        jnp.broadcast_to(shard[None], (size, *shard.shape)), axis, 0, 0, tiled=True
    )


def gathered_copies(shard, axis, dim):
    return laid_out(from_everyone(shard, axis), dim)


def fold_with(panel, piece):
    return jnp.einsum("htab,tgbc->hgac", panel, piece, preferred_element_type=jnp.float32)


def clique_filter(density, block_cols, mixing, row_start):
    row_count = density.shape[0]
    width = density.shape[2]
    groups_here = row_count // GS
    first_group = row_start // GS
    leaders = lax.dynamic_slice_in_dim(block_cols[:GS], first_group, groups_here, 1)
    ordered = density[:, 0][(leaders - row_start).reshape(-1)]
    ordered = ordered.reshape(GS, groups_here, 1, width, width)
    arrived = lax.all_to_all(ordered, "inner", split_axis=0, concat_axis=2, tiled=True)
    blocks = arrived[0]
    slot_count = blocks.shape[1]
    slot_start = lax.axis_index("col") * slot_count
    density_panel = gathered_copies(blocks, "col", 1)
    square = fold_with(density_panel, lax.all_gather(blocks, "row", axis=0, tiled=True)).astype(
        jnp.bfloat16
    )
    group_ids = first_group + jnp.arange(groups_here, dtype=jnp.int32)
    slot_ids = slot_start + jnp.arange(slot_count, dtype=jnp.int32)
    on_diagonal = (group_ids[:, None] == slot_ids[None, :]).astype(jnp.float32)
    identity = jnp.eye(width, dtype=jnp.float32)
    mixer_blocks = (
        mixing[0] * on_diagonal[:, :, None, None] * identity
        + mixing[1] * blocks.astype(jnp.float32)
        + mixing[2] * square.astype(jnp.float32)
    ).astype(jnp.bfloat16)
    square_panel = gathered_copies(square, "col", 1)
    filtered = fold_with(
        square_panel, lax.all_gather(mixer_blocks, "row", axis=0, tiled=True)
    ).astype(jnp.bfloat16)
    returned = lax.all_to_all(filtered[None], "inner", split_axis=2, concat_axis=0, tiled=True)
    regrouped = returned.reshape(GS * groups_here, 1, width, width)
    local_rows = row_start + jnp.arange(row_count, dtype=jnp.int32)
    clique_ids = lax.dynamic_slice_in_dim(block_cols[:, 0], row_start, row_count, 0)
    positions = clique_ids * groups_here + (local_rows // GS - first_group)
    return regrouped[positions]


def body(density, block_cols, mixing):
    row_count = density.shape[0]
    row_start = lax.axis_index("row") * row_count
    return clique_filter(density, block_cols, mixing, row_start)


def solution(mesh):
    in_specs = (P("row", ("col", "inner"), None, None), P(), P())
    out_specs = P("row", ("col", "inner"), None, None)
    return jax.shard_map(body, mesh=mesh, in_specs=in_specs, out_specs=out_specs, check_vma=False)
```

profile of v0, /device:TPU:1, one launch (start us, length us, event | category | flops | bytes accessed | tf_op | source)
XLA Modules:
  0.0 174.0 jit_solution(14277715915551514343)
XLA Ops:
  6.5 0.0 copy-start
  6.5 0.0 all-gather.6.cloned.1.call-start
  6.5 0.8 fusion.6
  7.3 0.3 copy-done
  7.6 0.6 gather_fusion
  8.2 0.2 copy.15
  8.4 13.4 %all_to_all.28 = bf16[4,1,1,256,256]{3,4,2,1,0:T(8,128)(2,1)S(1)} all-to-all(bf16[4,1,1,256,256]{3,4,2,1,0:T(8,128)(2,1)S(1)} %copy.15), channel_id=1, replica_groups=mesh['row'=16,'col'=4,'inner'=4] {'inner'}, dimensions={0} | all-to-all | bytes 1048576 | tf_op jit(solution)/shard_map/all_to_all | solution.py:38
  21.8 1.0 copy.17
  22.8 0.0 all-gather.6.cloned.1.call-update
  22.8 0.2 copy.18
  23.0 1.6 broadcast_in_dim.11
  24.6 4.1 %all-to-all-start.1 = ((bf16[4,1,4,256,256]{4,3,2,1,0:T(8,128)(2,1)}), bf16[4,1,4,256,256]{4,3,2,1,0:T(8,128)(2,1)S(1)}, u32[]{:S(2)}, u32[]{:S(2)}) async-start(bf16[4,1,4,256,256]{4,3,2,1,0:T(8,128)(2,1)} %broadcast_in_dim.11), calls=%async_computation.1 | async-start | bytes 4194304 | tf_op jit(solution)/shard_map/all_to_all | solution.py:17
  28.8 0.0 all-gather.4.cloned.1.call-start
  28.8 0.0 copy-done.1
  28.8 0.6 fusion.8
  29.4 0.6 compare_select_fusion.2
  30.0 23.1 %all-to-all-done.1 = bf16[4,1,4,256,256]{4,3,2,1,0:T(8,128)(2,1)S(1)} async-done(((bf16[4,1,4,256,256]{4,3,2,1,0:T(8,128)(2,1)}), bf16[4,1,4,256,256]{4,3,2,1,0:T(8,128)(2,1)S(1)}, u32[]{:S(2)}, u32[]{:S(2)}) %all-to-all-start.1) | async-done | bytes 2097184 | tf_op jit(solution)/shard_map/all_to_all | solution.py:17
  53.1 28.2 %all-gather.6.cloned.1.call-done = bf16[64,1,1,256,256]{4,3,2,1,0:T(8,128)(2,1)} async-done(((bf16[4,1,1,256,256]{4,3,2,1,0:T(8,128)(2,1)}), bf16[64,1,1,256,256]{4,3,2,1,0:T(8,128)(2,1)}) %all-gather.6.cloned.1.call-update) | async-done | bytes 8388624 | tf_op jit(solution)/shard_map/all_gather | solution.py:43
  81.3 8.0 %fusion.4 = (bf16[1,4,256,256]{2,3,1,0:T(8,128)(2,1)}, bf16[4,256,256]{2,1,0:T(8,128)(2,1)}) fusion(bf16[4,1,1,256,256]{3,4,2,1,0:T(8,128)(2,1)S(1)} %all_to_all.28, f32[]{:T(128)} %bitcast.1, f32[]{:T(128)} %bitcast.7, f32[256,256]{0,1:T(8,128)S(1)} %fusion.5, f32[4]{0:T(128)S(1)} %compare_select_fusion.2, bf16[16,4,256,256]{3,2,1,0:T(8,128)(2,1)} %bitcast.69, ...), kind=kOutput, calls=%fused_computation.9 | convolution fusion | flops 2149842944 | bytes 12320792 | tf_op jit(solution)/shard_map/htab,tgbc->hgac/dot_general | solution.py:27
  89.3 2.1 %copy.20 = bf16[1,4,256,256]{3,2,1,0:T(8,128)(2,1)} copy(bf16[1,4,256,256]{2,3,1,0:T(8,128)(2,1)} %get-tuple-element.8) | data formatting | bytes 1048576 | tf_op jit(solution)/shard_map/convert_element_type | solution.py:54
  91.4 0.0 all-gather.4.cloned.1.call-update
  91.4 1.2 copy.21
  92.7 0.2 broadcast_in_dim.26
  92.9 29.6 %all_to_all.29 = bf16[4,1,4,256,256]{4,3,2,1,0:T(8,128)(2,1)S(1)} all-to-all(bf16[4,1,4,256,256]{4,3,2,1,0:T(8,128)(2,1)S(1)} %broadcast_in_dim.26), channel_id=1, replica_groups=mesh['row'=16,'col'=4,'inner'=4] {'col'}, dimensions={0} | all-to-all | bytes 4194304 | tf_op jit(solution)/shard_map/all_to_all | solution.py:17
  122.5 23.5 %all-gather.4.cloned.1.call-done = bf16[16,4,256,256]{3,2,1,0:T(8,128)(2,1)} async-done(((bf16[1,4,256,256]{3,2,1,0:T(8,128)(2,1)}), bf16[16,4,256,256]{3,2,1,0:T(8,128)(2,1)}) %all-gather.4.cloned.1.call-update) | async-done | bytes 8388624 | tf_op jit(solution)/shard_map/all_gather | solution.py:57
  146.0 6.5 %fusion.2 = bf16[1,1,4,256,256]{3,4,1,0,2:T(8,128)(2,1)} fusion(bf16[16,4,256,256]{3,2,1,0:T(8,128)(2,1)} %all-gather.4.cloned.1.call-done, bf16[16,256,256,1]{2,1,3,0:T(8,128)(2,1)S(1)} %bitcast.63), kind=kOutput, calls=%fused_computation.6 | convolution fusion | flops 2147745792 | bytes 11010048 | tf_op jit(solution)/shard_map/htab,tgbc->hgac/dot_general | solution.py:27
  152.5 4.0 %all-to-all-start.3 = ((bf16[1,1,4,256,256]{3,4,1,0,2:T(8,128)(2,1)}), bf16[1,1,4,256,256]{3,4,1,0,2:T(8,128)(2,1)S(1)}, u32[]{:S(2)}, u32[]{:S(2)}) async-start(bf16[1,1,4,256,256]{3,4,1,0,2:T(8,128)(2,1)} %fusion.2), calls=%async_computation.3 | async-start | bytes 1048576 | tf_op jit(solution)/shard_map/all_to_all | solution.py:59
  156.5 0.7 slice.19
  157.2 0.1 fusion.7
  157.3 8.2 %all-to-all-done.3 = bf16[1,1,4,256,256]{3,4,1,0,2:T(8,128)(2,1)S(1)} async-done(((bf16[1,1,4,256,256]{3,4,1,0,2:T(8,128)(2,1)}), bf16[1,1,4,256,256]{3,4,1,0,2:T(8,128)(2,1)S(1)}, u32[]{:S(2)}, u32[]{:S(2)}) %all-to-all-start.3) | async-done | bytes 524320 | tf_op jit(solution)/shard_map/all_to_all | solution.py:59
  165.6 0.6 gather_fusion.1
  166.1 1.0 copy.24
  (4 shorter events, 0.0 us)
Async XLA Ops:
  6.5 1.1 copy-start
  6.5 74.8 %all-gather.6.cloned.1.call-start = ((), (), s32[]{:S(2)}) async-start(), calls=%async_computation.5 | async-start | bytes 8912896 | tf_op jit(solution)/shard_map/all_gather | solution.py:43
  24.6 4.2 %copy-start.1 = (f32[3]{0:T(128)S(1)}, f32[3]{0:T(128)}, u32[]{:S(2)}) copy-start(f32[3]{0:T(128)} %param.5) | copy-start | bytes 40
  24.6 28.5 %all-to-all-start.1 = ((bf16[4,1,4,256,256]{4,3,2,1,0:T(8,128)(2,1)}), bf16[4,1,4,256,256]{4,3,2,1,0:T(8,128)(2,1)S(1)}, u32[]{:S(2)}, u32[]{:S(2)}) async-start(bf16[4,1,4,256,256]{4,3,2,1,0:T(8,128)(2,1)} %broadcast_in_dim.11), calls=%async_computation.1 | async-start | bytes 4194304 | tf_op jit(solution)/shard_map/all_to_all | solution.py:17
  28.8 117.2 %all-gather.4.cloned.1.call-start = ((), (), s32[]{:S(2)}) async-start(), calls=%async_computation.4 | async-start | bytes 8912896 | tf_op jit(solution)/shard_map/all_gather | solution.py:57
  152.5 13.0 %all-to-all-start.3 = ((bf16[1,1,4,256,256]{3,4,1,0,2:T(8,128)(2,1)}), bf16[1,1,4,256,256]{3,4,1,0,2:T(8,128)(2,1)S(1)}, u32[]{:S(2)}, u32[]{:S(2)}) async-start(bf16[1,1,4,256,256]{3,4,1,0,2:T(8,128)(2,1)} %fusion.2), calls=%async_computation.3 | async-start | bytes 1048576 | tf_op jit(solution)/shard_map/all_to_all | solution.py:59
Sparse Core Ops, SparseCore 0:
  23.0 58.3 all-gather.5
  91.5 54.3 all-gather.3
where the time goes:
time: 175 us; the launch traced here: 174 us
  waiting for transfers between devices  83 us (47%)
  blocking collectives  43.1 us (25%)
  matrix products  14.6 us (8%)
  between operations  13.5 us (8%)
  local copies, waits for them, and re-layouts  10.2 us (6%)
  starting transfers between devices  8.15 us (5%)
    all_to_all x1, blocking collectives, from_everyone(): lax.all_to_all(jnp.broadcast_to(shard[None], (size, *shard.shape)), axis,...  29.6 us
    all_gather x1, waiting for transfers between devices, clique_filter(): lax.all_gather(blocks, 'row', axis=0, tiled=True)  28.2 us
    all_gather x1, waiting for transfers between devices, clique_filter(): lax.all_gather(mixer_blocks, 'row', axis=0, tiled=True)  23.5 us
    all_to_all x1, waiting for transfers between devices, from_everyone(): lax.all_to_all(jnp.broadcast_to(shard[None], (size, *shard.shape)), axis,...  23.1 us
    dot_general x2, matrix products, fold_with(): jnp.einsum('htab,tgbc->hgac', panel, piece, preferred_element_type=jnp.fl...  14.6 us
    all_to_all x1, blocking collectives, clique_filter(): lax.all_to_all(ordered, 'inner', split_axis=0, concat_axis=2, tiled=True)  13.4 us
    all_to_all x1, waiting for transfers between devices, clique_filter(): lax.all_to_all(filtered[None], 'inner', split_axis=2, concat_axis=0, tile...  8.25 us
    all_to_all x1, starting transfers between devices, from_everyone(): lax.all_to_all(jnp.broadcast_to(shard[None], (size, *shard.shape)), axis,...  4.14 us
  transfers between devices with their start and end apart: 4, of which 4 were waited for; matrix products, arithmetic and copies ran while one was open for 3% of the time, Pallas kernels for 0%

commit v1 on v0

v1 whole, which is shorter than its diff:
```python
import jax
import jax.numpy as jnp
from jax import lax
from jax.experimental import pallas as pl
from jax.experimental.pallas import tpu as pltpu
from jax.sharding import PartitionSpec as P


AXES = ("row", "col", "inner")
CORES = 2
NC = 4
PAIR = NC // 2
B = 256
RING8 = (0, -1, -2, -3, -4, 1, 2, 3)
RING4 = (-1, 1, -2)
LINES = 1 + 2 * len(RING4)
LEFTS = LINES + 12
RIGHTS = 2 * len(RING8)


def permutation(sizes, move):
    rows, cols, inners = sizes
    pairs = []
    for row in range(rows):
        for col in range(cols):
            for inner in range(inners):
                z, core = divmod(row, CORES)
                sign = 1 if core == 0 else -1
                dz, dx, dy, flip = move(sign)
                to_row = (z + dz) % (rows // CORES) * CORES + (core + flip) % CORES
                to = (to_row * cols + (col + dx) % cols) * inners + (inner + dy) % inners
                pairs.append(((row * cols + col) * inners + inner, to))
    return pairs


def product_kernel(*refs):
    cols_ref, mix_ref, own_ref = refs[:3]
    left, right = refs[3 : 3 + LEFTS], refs[3 + LEFTS : 3 + LEFTS + RIGHTS]
    s_ref, m_ref, lbuf, lsem = refs[3 + LEFTS + RIGHTS :]
    row = lax.axis_index("row")
    x = lax.axis_index("col")
    y = lax.axis_index("inner")
    zs = lax.axis_size("row") // CORES
    xs = lax.axis_size("col")
    ys = lax.axis_size("inner")
    z = row // CORES
    core = row % CORES
    sign = 1 - 2 * core
    weight = jnp.where(row == x * ys + y, mix_ref[0], 0.0)

    def local(c, u):
        return cols_ref[c, u] - NC * u

    @pl.loop(0, NC)
    def _(c):
        a = local(c, row)

        def place(src, dx, dy):
            g = lax.rem(x + dx * sign + xs, xs) * ys + lax.rem(y + dy * sign + ys, ys)
            pltpu.make_async_copy(src, lbuf.at[c, g], lsem.at[c]).start()

        place(left[0].at[a], 0, 0)
        for i, off in enumerate(RING4):
            place(left[1 + i].at[a], off, 0)
            place(left[4 + i].at[a], 0, off)

        @pl.when(a < PAIR)
        def _():
            for i, off in enumerate(RING4):
                place(left[7 + i].at[a], RING4[0], off)
                place(left[7 + i].at[PAIR + a], RING4[1], off)
                place(left[13 + i].at[a], RING4[2], off)

        @pl.when(a >= PAIR)
        def _():
            for i, off in enumerate(RING4):
                place(left[10 + i].at[a - PAIR], off, RING4[0])
                place(left[10 + i].at[a], off, RING4[1])
                place(left[16 + i].at[a - PAIR], off, RING4[2])

    @pl.loop(0, NC)
    def _(c):
        pltpu.make_async_copy(lbuf.at[c], lbuf.at[c], lsem.at[c]).wait()
        total = jnp.zeros((B, B), jnp.float32)
        for side in range(CORES):
            s = sign if side == 0 else -sign
            k = core if side == 0 else 1 - core
            for i, off in enumerate(RING8):
                u = lax.rem(z + off * s + zs, zs) * CORES + k
                total += jnp.dot(
                    lbuf[c, u],
                    right[side * len(RING8) + i][local(c, u)],
                    preferred_element_type=jnp.float32,
                )
        square = total.astype(jnp.bfloat16)
        a = local(c, row)
        s_ref[a] = square
        eye = lax.broadcasted_iota(jnp.int32, (B, B), 0) == lax.broadcasted_iota(
            jnp.int32, (B, B), 1
        )
        m_ref[a] = (
            jnp.where(eye, weight, 0.0)
            + mix_ref[1] * own_ref[a].astype(jnp.float32)
            + mix_ref[2] * square.astype(jnp.float32)
        ).astype(jnp.bfloat16)


def product(block_cols, mixing, own, left, right):
    tile = jax.ShapeDtypeStruct(own.shape, own.dtype)
    vmem = pl.BlockSpec(memory_space=pltpu.VMEM)
    depth = len(right) * B
    return pl.pallas_call(
        product_kernel,
        out_shape=(tile, tile),
        in_specs=[pl.BlockSpec(memory_space=pltpu.SMEM)] * 2
        + [vmem]
        + [pl.BlockSpec(memory_space=pl.ANY)] * len(left)
        + [vmem] * len(right),
        out_specs=(vmem, vmem),
        scratch_shapes=[
            pltpu.VMEM((NC, len(right), B, B), jnp.bfloat16),
            pltpu.SemaphoreType.DMA((NC,)),
        ],
        cost_estimate=pl.CostEstimate(
            flops=2 * NC * B * depth * B, bytes_accessed=4 * NC * B * depth, transcendentals=0
        ),
        name="product",
    )(block_cols, mixing, own, *left, *right)


def solution(mesh):
    sizes = tuple(mesh.shape[a] for a in AXES)
    moves = {
        "za": lambda s: (s, 0, 0, 0),
        "zb": lambda s: (-s, 0, 0, 0),
        "xa": lambda s: (0, s, 0, 0),
        "xb": lambda s: (0, -s, 0, 0),
        "ya": lambda s: (0, 0, s, 0),
        "yb": lambda s: (0, 0, -s, 0),
        "core": lambda s: (0, 0, 0, 1),
    }
    perms = {k: permutation(sizes, m) for k, m in moves.items()}

    def send(value, name):
        return lax.ppermute(value, AXES, perms[name])

    def ring4(tile, axis):
        a1 = send(tile, axis + "a")
        b1 = send(tile, axis + "b")
        return [a1, b1, send(a1, axis + "a")]

    def panels(row_tile, col_tile):
        along_x = ring4(row_tile, "x")
        along_y = ring4(row_tile, "y")
        forward, backward = [col_tile], [col_tile]
        for _ in range(4):
            forward.append(send(forward[-1], "za"))
        for _ in range(3):
            backward.append(send(backward[-1], "zb"))
        own = forward + backward[1:]
        corners = ring4(jnp.concatenate([t[:PAIR] for t in along_x[:2]]), "y")
        corners += ring4(jnp.concatenate([t[PAIR:] for t in along_y[:2]]), "x")
        corners += ring4(along_x[2][:PAIR], "y")
        corners += ring4(along_y[2][PAIR:], "x")
        partner = [send(t, "core") for t in own]
        return [row_tile] + along_x + along_y + corners, own + partner

    def body(density, block_cols, mixing):
        own = density[:, 0]

        def step(_, tiles):
            return product(block_cols, mixing, own, *panels(*tiles))

        return lax.fori_loop(0, 2, step, (own, own))[0][:, None]

    in_specs = (P("row", ("col", "inner"), None, None), P(), P())
    out_specs = P("row", ("col", "inner"), None, None)
    return jax.shard_map(body, mesh=mesh, in_specs=in_specs, out_specs=out_specs, check_vma=False)
```

time: 175 us -> 198 us (1.13)
  starting transfers between devices: 8.15 us -> 120 us
  blocking collectives: 43.1 us -> 0 us
  waiting for transfers between devices: 83 us -> 54.1 us
  Pallas kernels: 0 us -> 16 us
  matrix products: 14.6 us -> 0 us
  between operations: 13.5 us -> 0.02 us
  local copies, waits for them, and re-layouts: 10.2 us -> 6.5 us
    ppermute x0 -> x66, starting transfers between devices: none -> 120 us  [send(): return lax.ppermute(value, AXES, perms[name])]
    ppermute x0 -> x66, waiting for transfers between devices: none -> 54.1 us  [send(): return lax.ppermute(value, AXES, perms[name])]
    all_gather x2 -> x0, waiting for transfers between devices: 51.7 us -> none  [the longest x1 28.2 us: clique_filter(): lax.all_gather(blocks, 'row', axis=0, tiled=True)]
    all_to_all x2 -> x0, blocking collectives: 43.1 us -> none  [the longest x1 29.6 us: from_everyone(): lax.all_to_all(jnp.broadcast_to(shard[None], (size, *shard.shape)), axis,...]
    all_to_all x2 -> x0, waiting for transfers between devices: 31.3 us -> none  [the longest x1 23.1 us: from_everyone(): lax.all_to_all(jnp.broadcast_to(shard[None], (size, *shard.shape)), axis,...]
    pallas_call x0 -> x2, Pallas kernels: none -> 16 us  [product(): pl.pallas_call(product_kernel, out_shape=(tile, tile), in_specs=[pl.Block...]
    dot_general x2 -> x0, matrix products: 14.6 us -> none  [fold_with(): jnp.einsum('htab,tgbc->hgac', panel, piece, preferred_element_type=jnp.fl...]
    all_to_all x2 -> x0, starting transfers between devices: 8.15 us -> none  [the longest x1 4.14 us: from_everyone(): lax.all_to_all(jnp.broadcast_to(shard[None], (size, *shard.shape)), axis,...]
  transfers between devices with their start and end apart: 4 -> 66, of which waited for: 4 -> 22; matrix products, arithmetic and copies ran while one was open for 3% -> 0% of each run, Pallas kernels for 0% -> 0%
where the time goes in v1:
time: 198 us
  starting transfers between devices  120 us (61%)
  waiting for transfers between devices  54.1 us (27%)
  Pallas kernels  16 us (8%)
  local copies, waits for them, and re-layouts  6.5 us (3%)
    ppermute x66, starting transfers between devices, send(): return lax.ppermute(value, AXES, perms[name])  120 us
    ppermute x66, waiting for transfers between devices, send(): return lax.ppermute(value, AXES, perms[name])  54.1 us
    pallas_call x2, Pallas kernels, product(): pl.pallas_call(product_kernel, out_shape=(tile, tile), in_specs=[pl.Block...  16 us
  transfers between devices with their start and end apart: 66, of which 22 were waited for; matrix products, arithmetic and copies ran while one was open for 0% of the time, Pallas kernels for 0%

profile of v1, /device:TPU:1, one launch (start us, length us, event | category | flops | bytes accessed | tf_op | source)
XLA Modules:
  0.0 197.5 jit_solution(3919412696613648464)
XLA Ops:
  2.6 194.1 %while.12 = (s32[]{:T(128)}, bf16[4,256,256]{2,1,0:T(8,128)(2,1)S(1)}, bf16[4,256,256]{2,1,0:T(8,128)(2,1)S(1)}, s32[64,16]{1,0:T(8,128)S(1)}, f32[3]{0:T(128)S(1)}, /*index=5*/bf16[4,256,256]{2,1,0:T(8,128)(2,1)}, s32[]{:T(128)}) while((s32[]{:T(128)}, bf16[4,256,256]{2,1,0:T(8,128)(2,1)S(1)}, bf16[4,256,256]{2,1,0:T(8,128)(2,1)S(1)}, ...), condition=%wide.region_1.0_spmd, body=%wide.region_0.0_spmd.sunk | while | flops 2148007936 | bytes 139724880 | solution.py:174
  2.7 6.5 %collective-permute-start.18 = (bf16[4,256,256]{2,1,0:T(8,128)(2,1)S(1)}, bf16[4,256,256]{2,1,0:T(8,128)(2,1)S(1)}, u32[]{:S(2)}, u32[]{:S(2)}) collective-permute-start(bf16[4,256,256]{2,1,0:T(8,128)(2,1)S(1)} %copy.16.refs_22_), channel_id=1, source_target_pairs={{0,32},{1,33},{2,34},{3,35},{4,36},{5,37},{6,38},{7,39},{8,40},{9,... | collective-permute-start | bytes 1572872 | tf_op jit(solution)/shard_map/while/body/eval_jaxpr/ppermute | solution.py:145
  12.0 7.2 %collective-permute-done.18.refs_23_ = bf16[4,256,256]{2,1,0:T(8,128)(2,1)S(1)} collective-permute-done((bf16[4,256,256]{2,1,0:T(8,128)(2,1)S(1)}, bf16[4,256,256]{2,1,0:T(8,128)(2,1)S(1)}, u32[]{:S(2)}, u32[]{:S(2)}) %collective-permute-start.18) | collective-permute-done | bytes 524320 | tf_op jit(solution)/shard_map/while/body/eval_jaxpr/ppermute | solution.py:145
  24.2 3.4 %collective-permute-start.19 = (bf16[4,256,256]{2,1,0:T(8,128)(2,1)S(1)}, bf16[4,256,256]{2,1,0:T(8,128)(2,1)S(1)}, u32[]{:S(2)}, u32[]{:S(2)}) collective-permute-start(bf16[4,256,256]{2,1,0:T(8,128)(2,1)S(1)} %collective-permute-done.18.refs_23_), channel_id=1, source_target_pairs={{0,32},{1,33},{2,34},{3,35},{4,36},{5,37},{6,38},{7,39},{8,40},{9,... | collective-permute-start | bytes 1572872 | tf_op jit(solution)/shard_map/while/body/eval_jaxpr/ppermute | solution.py:145
  29.1 4.3 %collective-permute-done.3.refs_7_ = bf16[4,256,256]{2,1,0:T(8,128)(2,1)S(1)} collective-permute-done((bf16[4,256,256]{2,1,0:T(8,128)(2,1)S(1)}, bf16[4,256,256]{2,1,0:T(8,128)(2,1)S(1)}, u32[]{:S(2)}, u32[]{:S(2)}) %collective-permute-start.3) | collective-permute-done | bytes 524320 | tf_op jit(solution)/shard_map/while/body/eval_jaxpr/ppermute | solution.py:145
  42.0 3.1 %collective-permute-start.9 = (bf16[4,256,256]{2,1,0:T(8,128)(2,1)S(1)}, bf16[4,256,256]{2,1,0:T(8,128)(2,1)S(1)}, u32[]{:S(2)}, u32[]{:S(2)}) collective-permute-start(bf16[4,256,256]{2,1,0:T(8,128)(2,1)S(1)} %pad_maximum_fusion.5), channel_id=1, source_target_pairs={{0,4},{1,5},{2,6},{3,7},{4,8},{5,9},{6,10},{7,11},{8,12},{9,13},{1... | collective-permute-start | bytes 1572872 | tf_op jit(solution)/shard_map/while/body/eval_jaxpr/ppermute | solution.py:145
  45.1 4.3 %collective-permute-start.20 = (bf16[4,256,256]{2,1,0:T(8,128)(2,1)S(1)}, bf16[4,256,256]{2,1,0:T(8,128)(2,1)S(1)}, u32[]{:S(2)}, u32[]{:S(2)}) collective-permute-start(bf16[4,256,256]{2,1,0:T(8,128)(2,1)S(1)} %collective-permute-done.19.refs_24_), channel_id=1, source_target_pairs={{0,32},{1,33},{2,34},{3,35},{4,36},{5,37},{6,38},{7,39},{8,40},{9,... | collective-permute-start | bytes 1572872 | tf_op jit(solution)/shard_map/while/body/eval_jaxpr/ppermute | solution.py:145
  53.6 2.9 %collective-permute-start.12 = (bf16[2,256,256]{2,1,0:T(8,128)(2,1)S(1)}, bf16[2,256,256]{2,1,0:T(8,128)(2,1)}, u32[]{:S(2)}, u32[]{:S(2)}) collective-permute-start(bf16[2,256,256]{2,1,0:T(8,128)(2,1)S(1)} %slice.34), channel_id=1, source_target_pairs={{0,1},{1,2},{2,3},{3,0},{4,5},{5,6},{6,7},{7,4},{8,9},{9,10},{10,1... | collective-permute-start | bytes 786440 | tf_op jit(solution)/shard_map/while/body/eval_jaxpr/ppermute | solution.py:145
  56.5 6.3 %collective-permute-start.27 = (bf16[4,256,256]{2,1,0:T(8,128)(2,1)S(1)}, bf16[4,256,256]{2,1,0:T(8,128)(2,1)S(1)}, u32[]{:S(2)}, u32[]{:S(2)}) collective-permute-start(bf16[4,256,256]{2,1,0:T(8,128)(2,1)S(1)} %collective-permute-done.19.refs_24_), channel_id=1, source_target_pairs={{0,16},{1,17},{2,18},{3,19},{4,20},{5,21},{6,22},{7,23},{8,24},{9,... | collective-permute-start | bytes 1572872 | tf_op jit(solution)/shard_map/while/body/eval_jaxpr/ppermute | solution.py:145
  65.5 4.9 %collective-permute-start.31 = (bf16[4,256,256]{2,1,0:T(8,128)(2,1)S(1)}, bf16[4,256,256]{2,1,0:T(8,128)(2,1)S(1)}, u32[]{:S(2)}, u32[]{:S(2)}) collective-permute-start(bf16[4,256,256]{2,1,0:T(8,128)(2,1)S(1)} %collective-permute-done.23.refs_28_), channel_id=1, source_target_pairs={{0,16},{1,17},{2,18},{3,19},{4,20},{5,21},{6,22},{7,23},{8,24},{9,... | collective-permute-start | bytes 1572872 | tf_op jit(solution)/shard_map/while/body/eval_jaxpr/ppermute | solution.py:145
  70.9 2.7 %collective-permute-start.21 = (bf16[4,256,256]{2,1,0:T(8,128)(2,1)S(1)}, bf16[4,256,256]{2,1,0:T(8,128)(2,1)}, u32[]{:S(2)}, u32[]{:S(2)}) collective-permute-start(bf16[4,256,256]{2,1,0:T(8,128)(2,1)S(1)} %collective-permute-done.20.refs_25_), channel_id=1, source_target_pairs={{0,32},{1,33},{2,34},{3,35},{4,36},{5,37},{6,38},{7,39},{8,40},{9,... | collective-permute-start | bytes 1572872 | tf_op jit(solution)/shard_map/while/body/eval_jaxpr/ppermute | solution.py:145
  73.6 3.1 %collective-permute-start.8 = (bf16[4,256,256]{2,1,0:T(8,128)(2,1)S(1)}, bf16[4,256,256]{2,1,0:T(8,128)(2,1)S(1)}, u32[]{:S(2)}, u32[]{:S(2)}) collective-permute-start(bf16[4,256,256]{2,1,0:T(8,128)(2,1)S(1)} %collective-permute-done.6.refs_10_), channel_id=1, source_target_pairs={{0,1},{1,2},{2,3},{3,0},{4,5},{5,6},{6,7},{7,4},{8,9},{9,10},{10,1... | collective-permute-start | bytes 1572872 | tf_op jit(solution)/shard_map/while/body/eval_jaxpr/ppermute | solution.py:145
  76.9 7.7 %collective-permute-done.24.refs_29_ = bf16[4,256,256]{2,1,0:T(8,128)(2,1)} collective-permute-done((bf16[4,256,256]{2,1,0:T(8,128)(2,1)S(1)}, bf16[4,256,256]{2,1,0:T(8,128)(2,1)}, u32[]{:S(2)}, u32[]{:S(2)}) %collective-permute-start.24) | collective-permute-done | bytes 524320 | tf_op jit(solution)/shard_map/while/body/eval_jaxpr/ppermute | solution.py:145
  86.6 3.2 %collective-permute-start.14 = (bf16[2,256,256]{2,1,0:T(8,128)(2,1)}, bf16[2,256,256]{2,1,0:T(8,128)(2,1)}, u32[]{:S(2)}, u32[]{:S(2)}) collective-permute-start(bf16[2,256,256]{2,1,0:T(8,128)(2,1)} %collective-permute-done.12.refs_16_), channel_id=1, source_target_pairs={{0,1},{1,2},{2,3},{3,0},{4,5},{5,6},{6,7},{7,4},{8,9},{9,10},{10,1... | collective-permute-start | bytes 786440 | tf_op jit(solution)/shard_map/while/body/eval_jaxpr/ppermute | solution.py:145
  90.5 2.8 %collective-permute-done.14.refs_18_ = bf16[2,256,256]{2,1,0:T(8,128)(2,1)} collective-permute-done((bf16[2,256,256]{2,1,0:T(8,128)(2,1)}, bf16[2,256,256]{2,1,0:T(8,128)(2,1)}, u32[]{:S(2)}, u32[]{:S(2)}) %collective-permute-start.14) | collective-permute-done | bytes 262176 | tf_op jit(solution)/shard_map/while/body/eval_jaxpr/ppermute | solution.py:145
  95.4 8.0 %product.1 = (bf16[4,256,256]{2,1,0:T(8,128)(2,1)S(1)}, bf16[4,256,256]{2,1,0:T(8,128)(2,1)S(1)}) custom-call(s32[64,16]{1,0:T(8,128)S(1)} %get-tuple-element.116.refs_0_, f32[3]{0:T(128)S(1)} %get-tuple-element.117.refs_1_, bf16[4,256,256]{2,1,0:T(8,128)(2,1)S(1)} %copy-done.9, bf16[4,256,256]{2,1,0:T(8,128)(2,1)} %copy-done.1, ...), custom_call_target="tpu_custom_call" | custom-call | flops 2147483648 | bytes 16777216 | tf_op jit(solution)/shard_map/while/body/eval_jaxpr/product/pallas_call | solution.py:112
  105.2 2.7 %collective-permute-start = (bf16[4,256,256]{2,1,0:T(8,128)(2,1)S(1)}, bf16[4,256,256]{2,1,0:T(8,128)(2,1)S(1)}, u32[]{:S(2)}, u32[]{:S(2)}) collective-permute-start(bf16[4,256,256]{2,1,0:T(8,128)(2,1)S(1)} %copy.15.refs_3_), channel_id=1, source_target_pairs={{0,4},{1,5},{2,6},{3,7},{4,8},{5,9},{6,10},{7,11},{8,12},{9,13},{1... | collective-permute-start | bytes 1572872 | tf_op jit(solution)/shard_map/while/body/eval_jaxpr/ppermute | solution.py:145
  107.9 8.3 %collective-permute-done.18.refs_23_ = bf16[4,256,256]{2,1,0:T(8,128)(2,1)S(1)} collective-permute-done((bf16[4,256,256]{2,1,0:T(8,128)(2,1)S(1)}, bf16[4,256,256]{2,1,0:T(8,128)(2,1)S(1)}, u32[]{:S(2)}, u32[]{:S(2)}) %collective-permute-start.18) | collective-permute-done | bytes 524320 | tf_op jit(solution)/shard_map/while/body/eval_jaxpr/ppermute | solution.py:145
  116.2 2.7 %collective-permute-start.3 = (bf16[4,256,256]{2,1,0:T(8,128)(2,1)S(1)}, bf16[4,256,256]{2,1,0:T(8,128)(2,1)S(1)}, u32[]{:S(2)}, u32[]{:S(2)}) collective-permute-start(bf16[4,256,256]{2,1,0:T(8,128)(2,1)S(1)} %copy.15.refs_3_), channel_id=1, source_target_pairs={{0,1},{1,2},{2,3},{3,0},{4,5},{5,6},{6,7},{7,4},{8,9},{9,10},{10,1... | collective-permute-start | bytes 1572872 | tf_op jit(solution)/shard_map/while/body/eval_jaxpr/ppermute | solution.py:145
  119.1 3.7 %collective-permute-start.26 = (bf16[4,256,256]{2,1,0:T(8,128)(2,1)S(1)}, bf16[4,256,256]{2,1,0:T(8,128)(2,1)}, u32[]{:S(2)}, u32[]{:S(2)}) collective-permute-start(bf16[4,256,256]{2,1,0:T(8,128)(2,1)S(1)} %collective-permute-done.18.refs_23_), channel_id=1, source_target_pairs={{0,16},{1,17},{2,18},{3,19},{4,20},{5,21},{6,22},{7,23},{8,24},{9,... | collective-permute-start | bytes 1572872 | tf_op jit(solution)/shard_map/while/body/eval_jaxpr/ppermute | solution.py:145
  126.5 4.9 %collective-permute-start.2 = (bf16[4,256,256]{2,1,0:T(8,128)(2,1)S(1)}, bf16[4,256,256]{2,1,0:T(8,128)(2,1)S(1)}, u32[]{:S(2)}, u32[]{:S(2)}) collective-permute-start(bf16[4,256,256]{2,1,0:T(8,128)(2,1)S(1)} %collective-permute-done.refs_4_), channel_id=1, source_target_pairs={{0,4},{1,5},{2,6},{3,7},{4,8},{5,9},{6,10},{7,11},{8,12},{9,13},{1... | collective-permute-start | bytes 1572872 | tf_op jit(solution)/shard_map/while/body/eval_jaxpr/ppermute | solution.py:145
  131.4 2.7 %collective-permute-start.5 = (bf16[4,256,256]{2,1,0:T(8,128)(2,1)S(1)}, bf16[4,256,256]{2,1,0:T(8,128)(2,1)S(1)}, u32[]{:S(2)}, u32[]{:S(2)}) collective-permute-start(bf16[4,256,256]{2,1,0:T(8,128)(2,1)S(1)} %collective-permute-done.3.refs_7_), channel_id=1, source_target_pairs={{0,1},{1,2},{2,3},{3,0},{4,5},{5,6},{6,7},{7,4},{8,9},{9,10},{10,1... | collective-permute-start | bytes 1572872 | tf_op jit(solution)/shard_map/while/body/eval_jaxpr/ppermute | solution.py:145
  138.6 2.7 %collective-permute-start.9 = (bf16[4,256,256]{2,1,0:T(8,128)(2,1)S(1)}, bf16[4,256,256]{2,1,0:T(8,128)(2,1)S(1)}, u32[]{:S(2)}, u32[]{:S(2)}) collective-permute-start(bf16[4,256,256]{2,1,0:T(8,128)(2,1)S(1)} %pad_maximum_fusion.5), channel_id=1, source_target_pairs={{0,4},{1,5},{2,6},{3,7},{4,8},{5,9},{6,10},{7,11},{8,12},{9,13},{1... | collective-permute-start | bytes 1572872 | tf_op jit(solution)/shard_map/while/body/eval_jaxpr/ppermute | solution.py:145
  141.3 5.5 %collective-permute-start.20 = (bf16[4,256,256]{2,1,0:T(8,128)(2,1)S(1)}, bf16[4,256,256]{2,1,0:T(8,128)(2,1)S(1)}, u32[]{:S(2)}, u32[]{:S(2)}) collective-permute-start(bf16[4,256,256]{2,1,0:T(8,128)(2,1)S(1)} %collective-permute-done.19.refs_24_), channel_id=1, source_target_pairs={{0,32},{1,33},{2,34},{3,35},{4,36},{5,37},{6,38},{7,39},{8,40},{9,... | collective-permute-start | bytes 1572872 | tf_op jit(solution)/shard_map/while/body/eval_jaxpr/ppermute | solution.py:145
  146.8 3.7 %collective-permute-done.7.refs_11_ = bf16[4,256,256]{2,1,0:T(8,128)(2,1)S(1)} collective-permute-done((bf16[4,256,256]{2,1,0:T(8,128)(2,1)S(1)}, bf16[4,256,256]{2,1,0:T(8,128)(2,1)S(1)}, u32[]{:S(2)}, u32[]{:S(2)}) %collective-permute-start.7) | collective-permute-done | bytes 524320 | tf_op jit(solution)/shard_map/while/body/eval_jaxpr/ppermute | solution.py:145
  150.5 2.7 %collective-permute-start.12 = (bf16[2,256,256]{2,1,0:T(8,128)(2,1)S(1)}, bf16[2,256,256]{2,1,0:T(8,128)(2,1)}, u32[]{:S(2)}, u32[]{:S(2)}) collective-permute-start(bf16[2,256,256]{2,1,0:T(8,128)(2,1)S(1)} %slice.34), channel_id=1, source_target_pairs={{0,1},{1,2},{2,3},{3,0},{4,5},{5,6},{6,7},{7,4},{8,9},{9,10},{10,1... | collective-permute-start | bytes 786440 | tf_op jit(solution)/shard_map/while/body/eval_jaxpr/ppermute | solution.py:145
  159.7 3.6 %collective-permute-start.31 = (bf16[4,256,256]{2,1,0:T(8,128)(2,1)S(1)}, bf16[4,256,256]{2,1,0:T(8,128)(2,1)S(1)}, u32[]{:S(2)}, u32[]{:S(2)}) collective-permute-start(bf16[4,256,256]{2,1,0:T(8,128)(2,1)S(1)} %collective-permute-done.23.refs_28_), channel_id=1, source_target_pairs={{0,16},{1,17},{2,18},{3,19},{4,20},{5,21},{6,22},{7,23},{8,24},{9,... | collective-permute-start | bytes 1572872 | tf_op jit(solution)/shard_map/while/body/eval_jaxpr/ppermute | solution.py:145
  166.0 2.9 %collective-permute-start.8 = (bf16[4,256,256]{2,1,0:T(8,128)(2,1)S(1)}, bf16[4,256,256]{2,1,0:T(8,128)(2,1)S(1)}, u32[]{:S(2)}, u32[]{:S(2)}) collective-permute-start(bf16[4,256,256]{2,1,0:T(8,128)(2,1)S(1)} %collective-permute-done.6.refs_10_), channel_id=1, source_target_pairs={{0,1},{1,2},{2,3},{3,0},{4,5},{5,6},{6,7},{7,4},{8,9},{9,10},{10,1... | collective-permute-start | bytes 1572872 | tf_op jit(solution)/shard_map/while/body/eval_jaxpr/ppermute | solution.py:145
  168.9 2.9 %collective-permute-start.11 = (bf16[4,256,256]{2,1,0:T(8,128)(2,1)S(1)}, bf16[4,256,256]{2,1,0:T(8,128)(2,1)S(1)}, u32[]{:S(2)}, u32[]{:S(2)}) collective-permute-start(bf16[4,256,256]{2,1,0:T(8,128)(2,1)S(1)} %collective-permute-done.9.refs_13_), channel_id=1, source_target_pairs={{0,4},{1,5},{2,6},{3,7},{4,8},{5,9},{6,10},{7,11},{8,12},{9,13},{1... | collective-permute-start | bytes 1572872 | tf_op jit(solution)/shard_map/while/body/eval_jaxpr/ppermute | solution.py:145
  174.0 5.8 %collective-permute-start.32 = (bf16[4,256,256]{2,1,0:T(8,128)(2,1)}, bf16[4,256,256]{2,1,0:T(8,128)(2,1)}, u32[]{:S(2)}, u32[]{:S(2)}) collective-permute-start(bf16[4,256,256]{2,1,0:T(8,128)(2,1)} %collective-permute-done.24.refs_29_), channel_id=1, source_target_pairs={{0,16},{1,17},{2,18},{3,19},{4,20},{5,21},{6,22},{7,23},{8,24},{9,... | collective-permute-start | bytes 1572872 | tf_op jit(solution)/shard_map/while/body/eval_jaxpr/ppermute | solution.py:145
  179.9 3.0 %collective-permute-start.14 = (bf16[2,256,256]{2,1,0:T(8,128)(2,1)}, bf16[2,256,256]{2,1,0:T(8,128)(2,1)}, u32[]{:S(2)}, u32[]{:S(2)}) collective-permute-start(bf16[2,256,256]{2,1,0:T(8,128)(2,1)} %collective-permute-done.12.refs_16_), channel_id=1, source_target_pairs={{0,1},{1,2},{2,3},{3,0},{4,5},{5,6},{6,7},{7,4},{8,9},{9,10},{10,1... | collective-permute-start | bytes 786440 | tf_op jit(solution)/shard_map/while/body/eval_jaxpr/ppermute | solution.py:145
  188.7 8.0 %product.1 = (bf16[4,256,256]{2,1,0:T(8,128)(2,1)S(1)}, bf16[4,256,256]{2,1,0:T(8,128)(2,1)S(1)}) custom-call(s32[64,16]{1,0:T(8,128)S(1)} %get-tuple-element.116.refs_0_, f32[3]{0:T(128)S(1)} %get-tuple-element.117.refs_1_, bf16[4,256,256]{2,1,0:T(8,128)(2,1)S(1)} %copy-done.9, bf16[4,256,256]{2,1,0:T(8,128)(2,1)} %copy-done.1, ...), custom_call_target="tpu_custom_call" | custom-call | flops 2147483648 | bytes 16777216 | tf_op jit(solution)/shard_map/while/body/eval_jaxpr/product/pallas_call | solution.py:112
  (238 shorter events, 60.8 us)
Async XLA Ops:
  2.7 16.5 %collective-permute-start.18 = (bf16[4,256,256]{2,1,0:T(8,128)(2,1)S(1)}, bf16[4,256,256]{2,1,0:T(8,128)(2,1)S(1)}, u32[]{:S(2)}, u32[]{:S(2)}) collective-permute-start(bf16[4,256,256]{2,1,0:T(8,128)(2,1)S(1)} %copy.16.refs_22_), channel_id=1, source_target_pairs={{0,32},{1,33},{2,34},{3,35},{4,36},{5,37},{6,38},{7,39},{8,40},{9,... | collective-permute-start | bytes 1572872 | tf_op jit(solution)/shard_map/while/body/eval_jaxpr/ppermute | solution.py:145
  9.2 13.3 %collective-permute-start.22 = (bf16[4,256,256]{2,1,0:T(8,128)(2,1)S(1)}, bf16[4,256,256]{2,1,0:T(8,128)(2,1)S(1)}, u32[]{:S(2)}, u32[]{:S(2)}) collective-permute-start(bf16[4,256,256]{2,1,0:T(8,128)(2,1)S(1)} %copy.16.refs_22_), channel_id=1, source_target_pairs={{0,224},{1,225},{2,226},{3,227},{4,228},{5,229},{6,230},{7,231},{8... | collective-permute-start | bytes 1572872 | tf_op jit(solution)/shard_map/while/body/eval_jaxpr/ppermute | solution.py:145
  9.2 15.0 %collective-permute-start.1 = (bf16[4,256,256]{2,1,0:T(8,128)(2,1)S(1)}, bf16[4,256,256]{2,1,0:T(8,128)(2,1)S(1)}, u32[]{:S(2)}, u32[]{:S(2)}) collective-permute-start(bf16[4,256,256]{2,1,0:T(8,128)(2,1)S(1)} %copy.15.refs_3_), channel_id=1, source_target_pairs={{0,12},{1,13},{2,14},{3,15},{4,0},{5,1},{6,2},{7,3},{8,4},{9,5},{1... | collective-permute-start | bytes 1572872 | tf_op jit(solution)/shard_map/while/body/eval_jaxpr/ppermute | solution.py:145
  10.5 17.1 %collective-permute-start = (bf16[4,256,256]{2,1,0:T(8,128)(2,1)S(1)}, bf16[4,256,256]{2,1,0:T(8,128)(2,1)S(1)}, u32[]{:S(2)}, u32[]{:S(2)}) collective-permute-start(bf16[4,256,256]{2,1,0:T(8,128)(2,1)S(1)} %copy.15.refs_3_), channel_id=1, source_target_pairs={{0,4},{1,5},{2,6},{3,7},{4,8},{5,9},{6,10},{7,11},{8,12},{9,13},{1... | collective-permute-start | bytes 1572872 | tf_op jit(solution)/shard_map/while/body/eval_jaxpr/ppermute | solution.py:145
  22.5 13.4 %collective-permute-start.26 = (bf16[4,256,256]{2,1,0:T(8,128)(2,1)S(1)}, bf16[4,256,256]{2,1,0:T(8,128)(2,1)}, u32[]{:S(2)}, u32[]{:S(2)}) collective-permute-start(bf16[4,256,256]{2,1,0:T(8,128)(2,1)S(1)} %collective-permute-done.18.refs_23_), channel_id=1, source_target_pairs={{0,16},{1,17},{2,18},{3,19},{4,20},{5,21},{6,22},{7,23},{8,24},{9,... | collective-permute-start | bytes 1572872 | tf_op jit(solution)/shard_map/while/body/eval_jaxpr/ppermute | solution.py:145
  24.2 14.4 %collective-permute-start.19 = (bf16[4,256,256]{2,1,0:T(8,128)(2,1)S(1)}, bf16[4,256,256]{2,1,0:T(8,128)(2,1)S(1)}, u32[]{:S(2)}, u32[]{:S(2)}) collective-permute-start(bf16[4,256,256]{2,1,0:T(8,128)(2,1)S(1)} %collective-permute-done.18.refs_23_), channel_id=1, source_target_pairs={{0,32},{1,33},{2,34},{3,35},{4,36},{5,37},{6,38},{7,39},{8,40},{9,... | collective-permute-start | bytes 1572872 | tf_op jit(solution)/shard_map/while/body/eval_jaxpr/ppermute | solution.py:145
  38.6 13.4 %collective-permute-start.7 = (bf16[4,256,256]{2,1,0:T(8,128)(2,1)S(1)}, bf16[4,256,256]{2,1,0:T(8,128)(2,1)S(1)}, u32[]{:S(2)}, u32[]{:S(2)}) collective-permute-start(bf16[4,256,256]{2,1,0:T(8,128)(2,1)S(1)} %pad_maximum_fusion.4), channel_id=1, source_target_pairs={{0,3},{1,0},{2,1},{3,2},{4,7},{5,4},{6,5},{7,6},{8,11},{9,8},{10,9... | collective-permute-start | bytes 1572872 | tf_op jit(solution)/shard_map/while/body/eval_jaxpr/ppermute | solution.py:145
  38.8 14.9 %collective-permute-start.6 = (bf16[4,256,256]{2,1,0:T(8,128)(2,1)S(1)}, bf16[4,256,256]{2,1,0:T(8,128)(2,1)S(1)}, u32[]{:S(2)}, u32[]{:S(2)}) collective-permute-start(bf16[4,256,256]{2,1,0:T(8,128)(2,1)S(1)} %pad_maximum_fusion.4), channel_id=1, source_target_pairs={{0,1},{1,2},{2,3},{3,0},{4,5},{5,6},{6,7},{7,4},{8,9},{9,10},{10,1... | collective-permute-start | bytes 1572872 | tf_op jit(solution)/shard_map/while/body/eval_jaxpr/ppermute | solution.py:145
  41.4 15.1 %collective-permute-start.10 = (bf16[4,256,256]{2,1,0:T(8,128)(2,1)S(1)}, bf16[4,256,256]{2,1,0:T(8,128)(2,1)S(1)}, u32[]{:S(2)}, u32[]{:S(2)}) collective-permute-start(bf16[4,256,256]{2,1,0:T(8,128)(2,1)S(1)} %pad_maximum_fusion.5), channel_id=1, source_target_pairs={{0,12},{1,13},{2,14},{3,15},{4,0},{5,1},{6,2},{7,3},{8,4},{9,5},{1... | collective-permute-start | bytes 1572872 | tf_op jit(solution)/shard_map/while/body/eval_jaxpr/ppermute | solution.py:145
  42.0 20.8 %collective-permute-start.9 = (bf16[4,256,256]{2,1,0:T(8,128)(2,1)S(1)}, bf16[4,256,256]{2,1,0:T(8,128)(2,1)S(1)}, u32[]{:S(2)}, u32[]{:S(2)}) collective-permute-start(bf16[4,256,256]{2,1,0:T(8,128)(2,1)S(1)} %pad_maximum_fusion.5), channel_id=1, source_target_pairs={{0,4},{1,5},{2,6},{3,7},{4,8},{5,9},{6,10},{7,11},{8,12},{9,13},{1... | collective-permute-start | bytes 1572872 | tf_op jit(solution)/shard_map/while/body/eval_jaxpr/ppermute | solution.py:145
  45.1 25.8 %collective-permute-start.20 = (bf16[4,256,256]{2,1,0:T(8,128)(2,1)S(1)}, bf16[4,256,256]{2,1,0:T(8,128)(2,1)S(1)}, u32[]{:S(2)}, u32[]{:S(2)}) collective-permute-start(bf16[4,256,256]{2,1,0:T(8,128)(2,1)S(1)} %collective-permute-done.19.refs_24_), channel_id=1, source_target_pairs={{0,32},{1,33},{2,34},{3,35},{4,36},{5,37},{6,38},{7,39},{8,40},{9,... | collective-permute-start | bytes 1572872 | tf_op jit(solution)/shard_map/while/body/eval_jaxpr/ppermute | solution.py:145
  56.5 20.2 %collective-permute-start.27 = (bf16[4,256,256]{2,1,0:T(8,128)(2,1)S(1)}, bf16[4,256,256]{2,1,0:T(8,128)(2,1)S(1)}, u32[]{:S(2)}, u32[]{:S(2)}) collective-permute-start(bf16[4,256,256]{2,1,0:T(8,128)(2,1)S(1)} %collective-permute-done.19.refs_24_), channel_id=1, source_target_pairs={{0,16},{1,17},{2,18},{3,19},{4,20},{5,21},{6,22},{7,23},{8,24},{9,... | collective-permute-start | bytes 1572872 | tf_op jit(solution)/shard_map/while/body/eval_jaxpr/ppermute | solution.py:145
  70.9 13.7 %collective-permute-start.24 = (bf16[4,256,256]{2,1,0:T(8,128)(2,1)S(1)}, bf16[4,256,256]{2,1,0:T(8,128)(2,1)}, u32[]{:S(2)}, u32[]{:S(2)}) collective-permute-start(bf16[4,256,256]{2,1,0:T(8,128)(2,1)S(1)} %collective-permute-done.23.refs_28_), channel_id=1, source_target_pairs={{0,224},{1,225},{2,226},{3,227},{4,228},{5,229},{6,230},{7,231},{8... | collective-permute-start | bytes 1572872 | tf_op jit(solution)/shard_map/while/body/eval_jaxpr/ppermute | solution.py:145
  70.9 14.5 %collective-permute-start.21 = (bf16[4,256,256]{2,1,0:T(8,128)(2,1)S(1)}, bf16[4,256,256]{2,1,0:T(8,128)(2,1)}, u32[]{:S(2)}, u32[]{:S(2)}) collective-permute-start(bf16[4,256,256]{2,1,0:T(8,128)(2,1)S(1)} %collective-permute-done.20.refs_25_), channel_id=1, source_target_pairs={{0,32},{1,33},{2,34},{3,35},{4,36},{5,37},{6,38},{7,39},{8,40},{9,... | collective-permute-start | bytes 1572872 | tf_op jit(solution)/shard_map/while/body/eval_jaxpr/ppermute | solution.py:145
  73.6 13.0 %collective-permute-start.8 = (bf16[4,256,256]{2,1,0:T(8,128)(2,1)S(1)}, bf16[4,256,256]{2,1,0:T(8,128)(2,1)S(1)}, u32[]{:S(2)}, u32[]{:S(2)}) collective-permute-start(bf16[4,256,256]{2,1,0:T(8,128)(2,1)S(1)} %collective-permute-done.6.refs_10_), channel_id=1, source_target_pairs={{0,1},{1,2},{2,3},{3,0},{4,5},{5,6},{6,7},{7,4},{8,9},{9,10},{10,1... | collective-permute-start | bytes 1572872 | tf_op jit(solution)/shard_map/while/body/eval_jaxpr/ppermute | solution.py:145
  76.7 13.0 %collective-permute-start.11 = (bf16[4,256,256]{2,1,0:T(8,128)(2,1)S(1)}, bf16[4,256,256]{2,1,0:T(8,128)(2,1)S(1)}, u32[]{:S(2)}, u32[]{:S(2)}) collective-permute-start(bf16[4,256,256]{2,1,0:T(8,128)(2,1)S(1)} %collective-permute-done.9.refs_13_), channel_id=1, source_target_pairs={{0,4},{1,5},{2,6},{3,7},{4,8},{5,9},{6,10},{7,11},{8,12},{9,13},{1... | collective-permute-start | bytes 1572872 | tf_op jit(solution)/shard_map/while/body/eval_jaxpr/ppermute | solution.py:145
  76.8 18.5 %collective-permute-start.28 = (bf16[4,256,256]{2,1,0:T(8,128)(2,1)S(1)}, bf16[4,256,256]{2,1,0:T(8,128)(2,1)}, u32[]{:S(2)}, u32[]{:S(2)}) collective-permute-start(bf16[4,256,256]{2,1,0:T(8,128)(2,1)S(1)} %collective-permute-done.20.refs_25_), channel_id=1, source_target_pairs={{0,16},{1,17},{2,18},{3,19},{4,20},{5,21},{6,22},{7,23},{8,24},{9,... | collective-permute-start | bytes 1572872 | tf_op jit(solution)/shard_map/while/body/eval_jaxpr/ppermute | solution.py:145
  104.0 15.1 %collective-permute-start.22 = (bf16[4,256,256]{2,1,0:T(8,128)(2,1)S(1)}, bf16[4,256,256]{2,1,0:T(8,128)(2,1)S(1)}, u32[]{:S(2)}, u32[]{:S(2)}) collective-permute-start(bf16[4,256,256]{2,1,0:T(8,128)(2,1)S(1)} %copy.16.refs_22_), channel_id=1, source_target_pairs={{0,224},{1,225},{2,226},{3,227},{4,228},{5,229},{6,230},{7,231},{8... | collective-permute-start | bytes 1572872 | tf_op jit(solution)/shard_map/while/body/eval_jaxpr/ppermute | solution.py:145
  105.1 17.7 %collective-permute-start.1 = (bf16[4,256,256]{2,1,0:T(8,128)(2,1)S(1)}, bf16[4,256,256]{2,1,0:T(8,128)(2,1)S(1)}, u32[]{:S(2)}, u32[]{:S(2)}) collective-permute-start(bf16[4,256,256]{2,1,0:T(8,128)(2,1)S(1)} %copy.15.refs_3_), channel_id=1, source_target_pairs={{0,12},{1,13},{2,14},{3,15},{4,0},{5,1},{6,2},{7,3},{8,4},{9,5},{1... | collective-permute-start | bytes 1572872 | tf_op jit(solution)/shard_map/while/body/eval_jaxpr/ppermute | solution.py:145
  105.2 17.7 %collective-permute-start = (bf16[4,256,256]{2,1,0:T(8,128)(2,1)S(1)}, bf16[4,256,256]{2,1,0:T(8,128)(2,1)S(1)}, u32[]{:S(2)}, u32[]{:S(2)}) collective-permute-start(bf16[4,256,256]{2,1,0:T(8,128)(2,1)S(1)} %copy.15.refs_3_), channel_id=1, source_target_pairs={{0,4},{1,5},{2,6},{3,7},{4,8},{5,9},{6,10},{7,11},{8,12},{9,13},{1... | collective-permute-start | bytes 1572872 | tf_op jit(solution)/shard_map/while/body/eval_jaxpr/ppermute | solution.py:145
  125.4 13.2 %collective-permute-start.23 = (bf16[4,256,256]{2,1,0:T(8,128)(2,1)S(1)}, bf16[4,256,256]{2,1,0:T(8,128)(2,1)S(1)}, u32[]{:S(2)}, u32[]{:S(2)}) collective-permute-start(bf16[4,256,256]{2,1,0:T(8,128)(2,1)S(1)} %collective-permute-done.22.refs_27_), channel_id=1, source_target_pairs={{0,224},{1,225},{2,226},{3,227},{4,228},{5,229},{6,230},{7,231},{8... | collective-permute-start | bytes 1572872 | tf_op jit(solution)/shard_map/while/body/eval_jaxpr/ppermute | solution.py:145
  135.3 15.2 %collective-permute-start.7 = (bf16[4,256,256]{2,1,0:T(8,128)(2,1)S(1)}, bf16[4,256,256]{2,1,0:T(8,128)(2,1)S(1)}, u32[]{:S(2)}, u32[]{:S(2)}) collective-permute-start(bf16[4,256,256]{2,1,0:T(8,128)(2,1)S(1)} %pad_maximum_fusion.4), channel_id=1, source_target_pairs={{0,3},{1,0},{2,1},{3,2},{4,7},{5,4},{6,5},{7,6},{8,11},{9,8},{10,9... | collective-permute-start | bytes 1572872 | tf_op jit(solution)/shard_map/while/body/eval_jaxpr/ppermute | solution.py:145
  135.4 15.1 %collective-permute-start.6 = (bf16[4,256,256]{2,1,0:T(8,128)(2,1)S(1)}, bf16[4,256,256]{2,1,0:T(8,128)(2,1)S(1)}, u32[]{:S(2)}, u32[]{:S(2)}) collective-permute-start(bf16[4,256,256]{2,1,0:T(8,128)(2,1)S(1)} %pad_maximum_fusion.4), channel_id=1, source_target_pairs={{0,1},{1,2},{2,3},{3,0},{4,5},{5,6},{6,7},{7,4},{8,9},{9,10},{10,1... | collective-permute-start | bytes 1572872 | tf_op jit(solution)/shard_map/while/body/eval_jaxpr/ppermute | solution.py:145
  138.6 14.6 %collective-permute-start.10 = (bf16[4,256,256]{2,1,0:T(8,128)(2,1)S(1)}, bf16[4,256,256]{2,1,0:T(8,128)(2,1)S(1)}, u32[]{:S(2)}, u32[]{:S(2)}) collective-permute-start(bf16[4,256,256]{2,1,0:T(8,128)(2,1)S(1)} %pad_maximum_fusion.5), channel_id=1, source_target_pairs={{0,12},{1,13},{2,14},{3,15},{4,0},{5,1},{6,2},{7,3},{8,4},{9,5},{1... | collective-permute-start | bytes 1572872 | tf_op jit(solution)/shard_map/while/body/eval_jaxpr/ppermute | solution.py:145
  138.6 17.1 %collective-permute-start.9 = (bf16[4,256,256]{2,1,0:T(8,128)(2,1)S(1)}, bf16[4,256,256]{2,1,0:T(8,128)(2,1)S(1)}, u32[]{:S(2)}, u32[]{:S(2)}) collective-permute-start(bf16[4,256,256]{2,1,0:T(8,128)(2,1)S(1)} %pad_maximum_fusion.5), channel_id=1, source_target_pairs={{0,4},{1,5},{2,6},{3,7},{4,8},{5,9},{6,10},{7,11},{8,12},{9,13},{1... | collective-permute-start | bytes 1572872 | tf_op jit(solution)/shard_map/while/body/eval_jaxpr/ppermute | solution.py:145
  141.3 24.1 %collective-permute-start.20 = (bf16[4,256,256]{2,1,0:T(8,128)(2,1)S(1)}, bf16[4,256,256]{2,1,0:T(8,128)(2,1)S(1)}, u32[]{:S(2)}, u32[]{:S(2)}) collective-permute-start(bf16[4,256,256]{2,1,0:T(8,128)(2,1)S(1)} %collective-permute-done.19.refs_24_), channel_id=1, source_target_pairs={{0,32},{1,33},{2,34},{3,35},{4,36},{5,37},{6,38},{7,39},{8,40},{9,... | collective-permute-start | bytes 1572872 | tf_op jit(solution)/shard_map/while/body/eval_jaxpr/ppermute | solution.py:145
  153.2 15.7 %collective-permute-start.27 = (bf16[4,256,256]{2,1,0:T(8,128)(2,1)S(1)}, bf16[4,256,256]{2,1,0:T(8,128)(2,1)S(1)}, u32[]{:S(2)}, u32[]{:S(2)}) collective-permute-start(bf16[4,256,256]{2,1,0:T(8,128)(2,1)S(1)} %collective-permute-done.19.refs_24_), channel_id=1, source_target_pairs={{0,16},{1,17},{2,18},{3,19},{4,20},{5,21},{6,22},{7,23},{8,24},{9,... | collective-permute-start | bytes 1572872 | tf_op jit(solution)/shard_map/while/body/eval_jaxpr/ppermute | solution.py:145
  165.3 14.5 %collective-permute-start.21 = (bf16[4,256,256]{2,1,0:T(8,128)(2,1)S(1)}, bf16[4,256,256]{2,1,0:T(8,128)(2,1)}, u32[]{:S(2)}, u32[]{:S(2)}) collective-permute-start(bf16[4,256,256]{2,1,0:T(8,128)(2,1)S(1)} %collective-permute-done.20.refs_25_), channel_id=1, source_target_pairs={{0,32},{1,33},{2,34},{3,35},{4,36},{5,37},{6,38},{7,39},{8,40},{9,... | collective-permute-start | bytes 1572872 | tf_op jit(solution)/shard_map/while/body/eval_jaxpr/ppermute | solution.py:145
  166.0 13.9 %collective-permute-start.8 = (bf16[4,256,256]{2,1,0:T(8,128)(2,1)S(1)}, bf16[4,256,256]{2,1,0:T(8,128)(2,1)S(1)}, u32[]{:S(2)}, u32[]{:S(2)}) collective-permute-start(bf16[4,256,256]{2,1,0:T(8,128)(2,1)S(1)} %collective-permute-done.6.refs_10_), channel_id=1, source_target_pairs={{0,1},{1,2},{2,3},{3,0},{4,5},{5,6},{6,7},{7,4},{8,9},{9,10},{10,1... | collective-permute-start | bytes 1572872 | tf_op jit(solution)/shard_map/while/body/eval_jaxpr/ppermute | solution.py:145
  168.9 14.0 %collective-permute-start.11 = (bf16[4,256,256]{2,1,0:T(8,128)(2,1)S(1)}, bf16[4,256,256]{2,1,0:T(8,128)(2,1)S(1)}, u32[]{:S(2)}, u32[]{:S(2)}) collective-permute-start(bf16[4,256,256]{2,1,0:T(8,128)(2,1)S(1)} %collective-permute-done.9.refs_13_), channel_id=1, source_target_pairs={{0,4},{1,5},{2,6},{3,7},{4,8},{5,9},{6,10},{7,11},{8,12},{9,13},{1... | collective-permute-start | bytes 1572872 | tf_op jit(solution)/shard_map/while/body/eval_jaxpr/ppermute | solution.py:145
  171.9 16.7 %collective-permute-start.28 = (bf16[4,256,256]{2,1,0:T(8,128)(2,1)S(1)}, bf16[4,256,256]{2,1,0:T(8,128)(2,1)}, u32[]{:S(2)}, u32[]{:S(2)}) collective-permute-start(bf16[4,256,256]{2,1,0:T(8,128)(2,1)S(1)} %collective-permute-done.20.refs_25_), channel_id=1, source_target_pairs={{0,16},{1,17},{2,18},{3,19},{4,20},{5,21},{6,22},{7,23},{8,24},{9,... | collective-permute-start | bytes 1572872 | tf_op jit(solution)/shard_map/while/body/eval_jaxpr/ppermute | solution.py:145
  174.0 14.6 %collective-permute-start.32 = (bf16[4,256,256]{2,1,0:T(8,128)(2,1)}, bf16[4,256,256]{2,1,0:T(8,128)(2,1)}, u32[]{:S(2)}, u32[]{:S(2)}) collective-permute-start(bf16[4,256,256]{2,1,0:T(8,128)(2,1)} %collective-permute-done.24.refs_29_), channel_id=1, source_target_pairs={{0,16},{1,17},{2,18},{3,19},{4,20},{5,21},{6,22},{7,23},{8,24},{9,... | collective-permute-start | bytes 1572872 | tf_op jit(solution)/shard_map/while/body/eval_jaxpr/ppermute | solution.py:145
  (91 other events, 1373.0 us)
